TPU v7x, 32 devices: a whole 2x2x4 slice. The times are simulated.
32 devices in a mesh: loop: 4 (over y, x), bulk: 8 (over z, core).
Axes of the slice: x: 2, y: 2, z: 4, core: 2. Of those that a mesh axis runs over, the one named last changes fastest.
Arguments:
- series: float32 [4224, 3072], P('loop', 'bulk'), may hold values from -64 to 64
Outputs:
- correlation: float32 [4, 1056, 4224], P(None, 'bulk', 'loop')
All inputs are finite; a program needn't handle non-finite values.
Results may differ from a plain program's by a relative error of at most 0.0011.
Values may be sent and summed in bfloat16 or wider, within the bound.
A program may use at most 64 MiB of HBM per device.

v0:
```python
import jax
import jax.numpy as jnp
from jax import lax
from jax.sharding import PartitionSpec as P

TIME = 3072
epsilon = 1e-06


def normalize(centered, square_total):
    return (centered * lax.rsqrt(square_total / TIME + epsilon)).astype(jnp.bfloat16)


def contract(first_operand, second_operand):
    product = lax.dot_general(
        first_operand, second_operand, (((1,), (1,)), ((), ())), preferred_element_type=jnp.float32
    )
    return product / TIME


def cycle_gather(own_rows):
    return lax.all_gather(own_rows, "loop", axis=0, tiled=True)


def on_device(series):
    share_rows = series.shape[0] // lax.axis_size("bulk")
    average = lax.psum(jnp.sum(series, axis=1, keepdims=True), "bulk") / TIME
    centered = series - average
    squares = lax.psum(jnp.sum(centered * centered, axis=1, keepdims=True), "bulk")
    zscore = normalize(centered, squares)
    row_series = lax.all_gather(zscore, "bulk", axis=1, tiled=True)
    own_rows = lax.dynamic_slice_in_dim(
        row_series, lax.axis_index("bulk") * share_rows, share_rows, 0
    )
    gathered = contract(cycle_gather(own_rows), row_series)
    return gathered.reshape(lax.axis_size("loop"), share_rows, series.shape[0])


def solution(mesh):
    placed = (P("loop", "bulk"),)
    return jax.shard_map(
        on_device, mesh=mesh, in_specs=placed, out_specs=P(None, "bulk", "loop"), check_vma=False
    )
```

profile of v0, /device:TPU:0, one launch (start us, length us, event | category | flops | bytes accessed | tf_op | source)
XLA Modules:
  0.0 174.9 jit_solution(680406850263193112)
XLA Ops:
  6.5 0.0 copy-start
  6.5 0.0 all-gather.4.cloned.1.call-start
  6.5 1.8 %reduce_sum.18 = f32[1056]{0:T(1024)S(1)} reduce(f32[1056,384]{1,0:T(8,128)} %param.1, f32[]{:T(128)} %constant.7.clone.1), dimensions={1}, to_apply=%region_0.0 | reduce | flops 404448 | bytes 1626244 | tf_op jit(solution)/shard_map/reduce_sum | solution.py:27
  8.3 18.3 %psum.14 = f32[1056,1]{0,1:T(1,128)S(1)} all-reduce(f32[1056,1]{0,1:T(1,128)S(1)} %broadcast_in_dim.6), channel_id=1, replica_groups=mesh['loop'=4,'bulk'=8] {'bulk'}, use_global_device_ids=true, to_apply=%region_1.0 | all-reduce | flops 1056 | bytes 8448 | tf_op jit(solution)/shard_map/psum | solution.py:27
  26.7 0.0 copy-done
  26.7 0.4 multiply_reduce_fusion
  27.1 13.9 %psum.15 = f32[1056,1]{0,1:T(1,128)S(1)} all-reduce(f32[1056,1]{0,1:T(1,128)S(1)} %broadcast_in_dim.7), channel_id=1, replica_groups=mesh['loop'=4,'bulk'=8] {'bulk'}, use_global_device_ids=true, to_apply=%region_3.0 | all-reduce | flops 1056 | bytes 8448 | tf_op jit(solution)/shard_map/psum | solution.py:29
  41.1 1.2 multiply_convert_fusion
  42.3 0.0 all-gather.4.cloned.1.call-update
  42.3 0.0 all-gather.6.cloned.1.call-start
  42.4 64.4 %all-gather.4.cloned.1.call-done = bf16[1056,3072]{1,0:T(8,128)(2,1)} async-done(((bf16[1056,384]{1,0:T(8,128)(2,1)}), bf16[1056,3072]{1,0:T(8,128)(2,1)}) %all-gather.4.cloned.1.call-update) | async-done | bytes 6488080 | tf_op jit(solution)/shard_map/all_gather | solution.py:31
  106.8 2.3 %dynamic-slice_bitcast_fusion = bf16[1,132,3072]{2,1,0:T(8,128)(2,1)} fusion(bf16[1056,3072]{1,0:T(8,128)(2,1)} %all-gather.4.cloned.1.call-done, s32[]{:T(128)S(6)} %select_n.3), kind=kLoop, calls=%fused_computation.3 | loop fusion | bytes 1622020
  109.0 0.0 all-gather.6.cloned.1.call-update
  109.1 44.2 %all-gather.6.cloned.1.call-done = bf16[4,132,3072]{2,1,0:T(8,128)(2,1)} async-done(((bf16[1,132,3072]{2,1,0:T(8,128)(2,1)}), bf16[4,132,3072]{2,1,0:T(8,128)(2,1)}) %all-gather.6.cloned.1.call-update) | async-done | bytes 3244048 | tf_op jit(solution)/shard_map/all_gather | solution.py:22
  153.3 2.3 %reshape.5 = bf16[528,3072]{1,0:T(8,128)(2,1)S(1)} reshape(bf16[4,132,3072]{2,1,0:T(8,128)(2,1)} %all-gather.6.cloned.1.call-done) | data formatting | bytes 6488064
  155.6 8.7 %convolution_multiply_fusion = f32[528,1056]{1,0:T(8,128)} fusion(bf16[528,3072]{1,0:T(8,128)(2,1)S(1)} %reshape.5, bf16[1056,3072]{1,0:T(8,128)(2,1)} %all-gather.4.cloned.1.call-done), kind=kOutput, calls=%fused_computation | convolution fusion | flops 3426255360 | bytes 11962368 | tf_op jit(solution)/shard_map/dot_general | solution.py:15
  164.2 1.8 %reshape.3 = f32[4,132,1056]{2,1,0:T(8,128)S(1)} reshape(f32[528,1056]{1,0:T(8,128)} %convolution_multiply_fusion) | data formatting | bytes 4460544 | tf_op jit(solution)/shard_map/reshape | solution.py:36
  166.0 2.1 %copy.4 = f32[4,132,1056]{2,0,1:T(4,128)} copy(f32[4,132,1056]{2,1,0:T(8,128)S(1)} %reshape.3) | data formatting | bytes 4460544 | tf_op jit(solution)/shard_map/reshape | solution.py:36
  (4 shorter events, 0.1 us)
Async XLA Ops:
  6.5 20.2 %copy-start = (f32[1056,384]{1,0:T(8,128)S(1)}, f32[1056,384]{1,0:T(8,128)}, u32[]{:S(2)}) copy-start(f32[1056,384]{1,0:T(8,128)} %param.1) | copy-start | bytes 4866052
  6.5 100.2 %all-gather.4.cloned.1.call-start = ((), (), s32[]{:S(2)}) async-start(), calls=%async_computation | async-start | bytes 7299072 | tf_op jit(solution)/shard_map/all_gather | solution.py:31
  42.3 110.9 %all-gather.6.cloned.1.call-start = ((), (), s32[]{:S(2)}) async-start(), calls=%async_computation.1 | async-start | bytes 4177920 | tf_op jit(solution)/shard_map/all_gather | solution.py:22
Sparse Core Ops, SparseCore 0:
  42.5 64.2 all-gather.3
  109.2 44.0 all-gather.5
where the time goes:
time: 175 us
  waiting for transfers between devices  109 us (62%)
  blocking collectives  32.3 us (18%)
  between operations  13.5 us (8%)
  matrix products  8.65 us (5%)
  local copies, waits for them, and re-layouts  8.41 us (5%)
  other arithmetic  3.46 us (2%)
    all_gather x1, waiting for transfers between devices, on_device(): row_series = lax.all_gather(zscore, 'bulk', axis=1, tiled=True)  64.4 us
    all_gather x1, waiting for transfers between devices, cycle_gather(): return lax.all_gather(own_rows, 'loop', axis=0, tiled=True)  44.2 us
    psum x1, blocking collectives, on_device(): average = lax.psum(jnp.sum(series, axis=1, keepdims=True), 'bulk') / TIME  18.3 us
    psum x1, blocking collectives, on_device(): lax.psum(jnp.sum(centered * centered, axis=1, keepdims=True), 'bulk')  13.9 us
    dot_general x1, matrix products, contract(): lax.dot_general(first_operand, second_operand, (((1,), (1,)), ((), ())),...  8.65 us
    unnamed x4, local copies, waits for them, and re-layouts  4.55 us
    reshape x2, local copies, waits for them, and re-layouts, on_device(): return gathered.reshape(lax.axis_size('loop'), share_rows, series.shape[0])  3.84 us
  transfers between devices with their start and end apart: 2, of which 2 were waited for; matrix products, arithmetic and copies ran while one was open for 0% of the time, Pallas kernels for 0%

commit v1 on v0

--- a/solution.py
+++ b/solution.py
@@ -19,7 +19,9 @@
 
 
 def cycle_gather(own_rows):
-    return lax.all_gather(own_rows, "loop", axis=0, tiled=True)
+    return jnp.concatenate(
+        lax.all_to_all(jnp.stack([own_rows] * lax.axis_size("loop")), "loop", 0, 0), axis=0
+    )
 
 
 def on_device(series):

time: 175 us -> 174 us (level)
  waiting for transfers between devices: 109 us -> 64.4 us
  blocking collectives: 32.3 us -> 75 us
    all_gather x1 -> x0, waiting for transfers between devices: 44.2 us -> none  [cycle_gather(): return lax.all_gather(own_rows, 'loop', axis=0, tiled=True)]
    all_to_all x0 -> x1, blocking collectives: none -> 42.7 us  [cycle_gather(): lax.all_to_all(jnp.stack([own_rows] * lax.axis_size('loop')), 'loop', 0, 0)]
    unnamed x4 -> x2, local copies, waits for them, and re-layouts: 4.55 us -> 0.01 us
    reshape x0 -> x1, local copies, waits for them, and re-layouts: none -> 2.05 us  [cycle_gather(): jnp.concatenate(lax.all_to_all(jnp.stack([own_rows] * lax.axis_size('loop...]
  transfers between devices with their start and end apart: 2 -> 1, of which waited for: 2 -> 1; matrix products, arithmetic and copies ran while one was open for 0% -> 0% of each run, Pallas kernels for 0% -> 0%
where the time goes in v1:
time: 174 us
  blocking collectives  75 us (43%)
  waiting for transfers between devices  64.4 us (37%)
  between operations  13.5 us (8%)
  matrix products  9.65 us (6%)
  local copies, waits for them, and re-layouts  7.68 us (4%)
  other arithmetic  3.46 us (2%)
    all_gather x1, waiting for transfers between devices, on_device(): row_series = lax.all_gather(zscore, 'bulk', axis=1, tiled=True)  64.4 us
    all_to_all x1, blocking collectives, cycle_gather(): lax.all_to_all(jnp.stack([own_rows] * lax.axis_size('loop')), 'loop', 0, 0)  42.7 us
    psum x1, blocking collectives, on_device(): average = lax.psum(jnp.sum(series, axis=1, keepdims=True), 'bulk') / TIME  18.3 us
    psum x1, blocking collectives, on_device(): lax.psum(jnp.sum(centered * centered, axis=1, keepdims=True), 'bulk')  13.9 us
    dot_general x1, matrix products, contract(): lax.dot_general(first_operand, second_operand, (((1,), (1,)), ((), ())),...  9.65 us
    reshape x2, local copies, waits for them, and re-layouts, on_device(): return gathered.reshape(lax.axis_size('loop'), share_rows, series.shape[0])  3.84 us
  transfers between devices with their start and end apart: 1, of which 1 were waited for; matrix products, arithmetic and copies ran while one was open for 0% of the time, Pallas kernels for 0%

profile of v1, /device:TPU:0, one launch (start us, length us, event | category | flops | bytes accessed | tf_op | source)
XLA Modules:
  0.0 173.7 jit_solution(8383527237116527347)
XLA Ops:
  6.5 0.0 copy-start
  6.5 0.0 all-gather.2.cloned.1.call-start
  6.5 1.8 %reduce_sum.18 = f32[1056]{0:T(1024)S(1)} reduce(f32[1056,384]{1,0:T(8,128)} %param.1, f32[]{:T(128)} %constant.7.clone.1), dimensions={1}, to_apply=%region_0.0 | reduce | flops 404448 | bytes 1626244 | tf_op jit(solution)/shard_map/reduce_sum | solution.py:29
  8.3 18.3 %psum.14 = f32[1056,1]{0,1:T(1,128)S(1)} all-reduce(f32[1056,1]{0,1:T(1,128)S(1)} %broadcast_in_dim.6), channel_id=1, replica_groups=mesh['loop'=4,'bulk'=8] {'bulk'}, use_global_device_ids=true, to_apply=%region_1.0 | all-reduce | flops 1056 | bytes 8448 | tf_op jit(solution)/shard_map/psum | solution.py:29
  26.7 0.0 copy-done
  26.7 0.4 multiply_reduce_fusion
  27.1 13.9 %psum.15 = f32[1056,1]{0,1:T(1,128)S(1)} all-reduce(f32[1056,1]{0,1:T(1,128)S(1)} %broadcast_in_dim.7), channel_id=1, replica_groups=mesh['loop'=4,'bulk'=8] {'bulk'}, use_global_device_ids=true, to_apply=%region_3.0 | all-reduce | flops 1056 | bytes 8448 | tf_op jit(solution)/shard_map/psum | solution.py:31
  41.1 1.2 multiply_convert_fusion
  42.3 0.0 all-gather.2.cloned.1.call-update
  42.3 64.4 %all-gather.2.cloned.1.call-done = bf16[1056,3072]{1,0:T(8,128)(2,1)} async-done(((bf16[1056,384]{1,0:T(8,128)(2,1)}), bf16[1056,3072]{1,0:T(8,128)(2,1)}) %all-gather.2.cloned.1.call-update) | async-done | bytes 6488080 | tf_op jit(solution)/shard_map/all_gather | solution.py:33
  106.8 1.4 constant_dynamic-slice_fusion
  108.1 0.4 stack.2
  108.6 42.7 %all_to_all.5 = bf16[4,132,3072]{2,1,0:T(8,128)(2,1)S(1)} all-to-all(bf16[4,132,3072]{2,1,0:T(8,128)(2,1)S(1)} %stack.2), channel_id=1, replica_groups=mesh['loop'=4,'bulk'=8] {'loop'}, dimensions={0} | all-to-all | bytes 6488064 | tf_op jit(solution)/shard_map/all_to_all | solution.py:23
  151.3 2.1 %reshape.8 = bf16[528,3072]{1,0:T(8,128)(2,1)} reshape(bf16[4,132,3072]{2,1,0:T(8,128)(2,1)S(1)} %all_to_all.5) | data formatting | bytes 6488064 | tf_op jit(solution)/shard_map/reshape | solution.py:22
  153.3 9.6 %convolution_multiply_fusion = f32[528,1056]{1,0:T(8,128)} fusion(bf16[528,3072]{1,0:T(8,128)(2,1)} %reshape.8, bf16[1056,3072]{1,0:T(8,128)(2,1)} %all-gather.2.cloned.1.call-done), kind=kOutput, calls=%fused_computation | convolution fusion | flops 3426255360 | bytes 11962368 | tf_op jit(solution)/shard_map/dot_general | solution.py:15
  163.0 1.8 %reshape.9 = f32[4,132,1056]{2,1,0:T(8,128)S(1)} reshape(f32[528,1056]{1,0:T(8,128)} %convolution_multiply_fusion) | data formatting | bytes 4460544 | tf_op jit(solution)/shard_map/reshape | solution.py:38
  164.8 2.1 %copy.3 = f32[4,132,1056]{2,0,1:T(4,128)} copy(f32[4,132,1056]{2,1,0:T(8,128)S(1)} %reshape.9) | data formatting | bytes 4460544 | tf_op jit(solution)/shard_map/reshape | solution.py:38
  (4 shorter events, 0.1 us)
Async XLA Ops:
  6.5 20.2 %copy-start = (f32[1056,384]{1,0:T(8,128)S(1)}, f32[1056,384]{1,0:T(8,128)}, u32[]{:S(2)}) copy-start(f32[1056,384]{1,0:T(8,128)} %param.1) | copy-start | bytes 4866052
  6.5 100.2 %all-gather.2.cloned.1.call-start = ((), (), s32[]{:S(2)}) async-start(), calls=%async_computation.1 | async-start | bytes 7299072 | tf_op jit(solution)/shard_map/all_gather | solution.py:33
Sparse Core Ops, SparseCore 0:
  42.5 64.2 all-gather.1
